TPU v7x, 32 devices: a whole 2x2x4 slice. The times are simulated.
32 devices in a mesh: rep: 2 (over x), fsdp: 16 (over z, y, core).
Axes of the slice: x: 2, y: 2, z: 4, core: 2. Of those that a mesh axis runs over, the one named last changes fastest.
Arguments:
- tokens: bfloat16 [4, 1024, 2048], P('rep', 'fsdp'), may hold values from -6 to 6
- segment_ids: int32 [4, 1024], P('rep', 'fsdp'), may hold values from 0 to 1, never falling along the last dimension, each value on 1 to 768 neighbouring positions
- norm_gains: bfloat16 [2048, 2], P('fsdp'), may hold values from 0.5 to 1.5
- attn_weight: bfloat16 [2048, 4608], P('fsdp'), may hold values from -0.79549513 to 0.79549513
- adapter: bfloat16 [2048, 768], P('fsdp'), may hold values from -0.125 to 0.125
- ffn_weight: bfloat16 [16384, 3, 2048], P('fsdp'), may hold values from -0.125 to 0.125
- ffn_adapter: bfloat16 [16384, 256], P('fsdp'), may hold values from -0.046875 to 0.046875
- cotangent: bfloat16 [4, 1024, 2048], P('rep', 'fsdp'), may hold values from -6 to 6
Outputs:
- block_output: bfloat16 [4, 1024, 2048], P('rep', 'fsdp')
- input_grad: bfloat16 [4, 1024, 2048], P('rep', 'fsdp')
- gains_grad: float32 [2048, 2], P('fsdp')
- attn_grad: float32 [2048, 4608], P('fsdp')
- adapter_grad: float32 [2048, 768], P('fsdp')
- ffn_grad: float32 [16384, 3, 2048], P('fsdp')
- ffn_adapter_grad: float32 [16384, 256], P('fsdp')
Inputs may be any that keep to these rules, and one draw needn't show every extreme that they name: `segment_ids`: in each sequence the ids never fall and each id of 0 to 1 marks one document of 1 to 768 tokens.
All inputs are finite; a program needn't handle non-finite values.
Results may differ from a plain program's by a relative error of at most 0.019.
Values may be sent and summed in bfloat16 or wider, within the bound.
A program may use at most 448 MiB of HBM per device.

v0:
```python
import jax
import jax.numpy as jnp
from jax import lax
from jax.sharding import PartitionSpec as P

HEADS = 8
HD = 256
RANK = 256
CHUNKS = 4
epsilon = 1e-06


def rms_scale(values, gain_col):
    return (
        values * lax.rsqrt(jnp.mean(values * values, axis=-1, keepdims=True) + epsilon) * gain_col
    )


def angles_of(positions):
    inverse_freq = 10000.0 ** (-2.0 * jnp.arange(HD // 2, dtype=jnp.float32) / HD)
    return positions.astype(jnp.float32)[..., None] * inverse_freq


def rotate(field_in, angles):
    half_dim = field_in.shape[-1] // 2
    cosine = jnp.cos(angles)
    sine_part = jnp.sin(angles)
    lower_half = field_in[..., :half_dim]
    upper_half = field_in[..., half_dim:]
    return jnp.concatenate(
        [
            lower_half * cosine - upper_half * sine_part,
            upper_half * cosine + lower_half * sine_part,
        ],
        axis=-1,
    )


def gelu_tanh(values):
    return jax.nn.gelu(values, approximate=True)


def contract(left_op, right_op, left_dim, right_dim):
    return lax.dot_general(
        left_op,
        right_op,
        (((left_dim,), (right_dim,)), ((), ())),
        preferred_element_type=jnp.float32,
    )


def batched(left_op, right_op, left_dim, right_dim):
    return lax.dot_general(
        left_op,
        right_op,
        (((left_dim,), (right_dim,)), ((0,), (0,))),
        preferred_element_type=jnp.float32,
    )


def low(values):
    return values.astype(jnp.bfloat16)


def gather_rows(values):
    return lax.all_gather(values, "fsdp", axis=values.ndim - 2, tiled=True)


def sum_rows(values):
    return lax.psum_scatter(values, "fsdp", scatter_dimension=1, tiled=True)


def swap_rep(values):
    return lax.ppermute(values, "rep", [(0, 1), (1, 0)])


def local(
    tokens, segment_ids, norm_gains, attn_weight, adapter, ffn_weight, ffn_adapter, cotangent
):
    micro, local_len, model_dim = tokens.shape
    shards = lax.axis_size("fsdp")
    me = lax.axis_index("fsdp")
    seq_len = local_len * shards
    offset = me * local_len
    count = micro * local_len
    every = micro * seq_len
    q_width = HEADS * HD
    kv_end = q_width + 2 * HD
    score_scale = HD ** (-0.5)
    hidden_cols = ffn_weight.shape[0]
    attn_rows = attn_weight.shape[0]
    seg_cols = count // attn_rows
    seg_block = low(segment_ids).reshape(attn_rows, seg_cols)
    spare = jnp.zeros((attn_rows, 128 - 2 - seg_cols), jnp.bfloat16)
    first = gather_rows(
        jnp.concatenate(
            [attn_weight[:, :kv_end], adapter[:, : 2 * RANK], norm_gains, seg_block, spare], axis=1
        )
    )
    second = gather_rows(jnp.concatenate([attn_weight[:, kv_end:], adapter[:, 2 * RANK :]], axis=1))
    extra = kv_end + 2 * RANK
    w_proj = first[:, :kv_end]
    a_q = first[:, kv_end : kv_end + RANK]
    bq_t = first[:, kv_end + RANK : extra]
    gain_two = first[:, extra : extra + 2].astype(jnp.float32)
    seg_all = first[:, extra + 2 : extra + 2 + seg_cols].reshape(shards, micro, local_len)
    seg_all = seg_all.transpose(1, 0, 2).reshape(micro, seq_len).astype(jnp.int32)
    w_out = second[:, :q_width]
    bd_t = second[:, q_width:]
    cot_all = gather_rows(cotangent).reshape(every, model_dim)
    hidden_in = tokens.reshape(count, model_dim).astype(jnp.float32)
    key_index = jnp.arange(seq_len, dtype=jnp.int32)
    query_index = offset + jnp.arange(local_len, dtype=jnp.int32)
    before = jnp.sum((seg_all[:, None, :] < segment_ids[:, :, None]).astype(jnp.int32), axis=2)
    angles = angles_of(query_index[None, :] - before).reshape(count, HD // 2)
    normed, norm_back_one = jax.vjp(rms_scale, hidden_in, gain_two[:, 0])
    normed_low = low(normed)
    normed_cols = lax.all_to_all(
        normed_low.reshape(micro, local_len, model_dim), "fsdp", 2, 1, tiled=True
    ).reshape(every, attn_rows)
    projected = contract(normed_low, w_proj, 1, 0)
    query_low = low(contract(normed_low, a_q, 1, 0))
    query_pre = projected[:, :q_width] + contract(query_low, bq_t, 1, 1)
    queries = low(rotate(query_pre.reshape(count, HEADS, HD), angles[:, None, :]))
    queries = queries.reshape(micro, local_len * HEADS, HD)
    keys_low = low(rotate(projected[:, q_width : q_width + HD], angles))
    values_low = low(projected[:, q_width + HD :])
    kv_all = gather_rows(
        jnp.concatenate([keys_low, values_low], axis=1).reshape(micro, local_len, 2 * HD)
    )
    keys_all = kv_all[..., :HD]
    values_all = kv_all[..., HD:]
    allowed = (
        (segment_ids[:, :, None] == seg_all[:, None, :])
        & (key_index[None, None, :] <= query_index[None, :, None])
    )[:, :, None, :]
    scores = (batched(queries, keys_all, 2, 2) * score_scale).reshape(
        micro, local_len, HEADS, seq_len
    )
    scores = jnp.where(allowed, scores, -1e30)
    top_score = jnp.max(scores, axis=-1, keepdims=True)
    exp_scores = jnp.exp(scores - top_score)
    weights = exp_scores / jnp.sum(exp_scores, axis=-1, keepdims=True)
    weights_low = low(weights).reshape(micro, local_len * HEADS, seq_len)
    context = low(batched(weights_low, values_all, 2, 1)).reshape(count, q_width)
    mixed_sum = hidden_in + contract(context, w_out, 1, 1)
    normed_two, norm_back_two = jax.vjp(rms_scale, mixed_sum, gain_two[:, 1])
    inputs_all = gather_rows(low(normed_two).reshape(micro, local_len, model_dim))
    inputs_all = inputs_all.reshape(every, model_dim)
    kept_all = gather_rows(
        jnp.concatenate([context, query_low], axis=1).reshape(micro, local_len, q_width + RANK)
    ).reshape(every, q_width + RANK)
    low_grad_all = low(contract(cot_all, bd_t, 1, 0))
    step = hidden_cols // CHUNKS
    hidden_parts, gate_parts, up_parts, ffn_parts, low_parts = ([], [], [], [], [])
    for at in range(CHUNKS):
        units = slice(at * step, (at + 1) * step)
        w_gate, w_up, w_down = (ffn_weight[units, j, :] for j in range(3))
        gate_pre = contract(inputs_all, w_gate, 1, 1)
        up_pre = contract(inputs_all, w_up, 1, 1)
        activated, gelu_back = jax.vjp(gelu_tanh, gate_pre)
        hidden_act = low(activated * up_pre)
        hidden_grad = contract(cot_all, w_down, 1, 1) + contract(
            low_grad_all, ffn_adapter[units], 1, 1
        )
        gate_grad = low(gelu_back(hidden_grad * up_pre)[0])
        up_grad = low(hidden_grad * activated)
        mine = low(
            jnp.stack(
                [
                    contract(gate_grad, inputs_all, 0, 0),
                    contract(up_grad, inputs_all, 0, 0),
                    contract(hidden_act, cot_all, 0, 0),
                ],
                axis=0,
            )
        )
        mine_low = low(contract(hidden_act, low_grad_all, 0, 0))
        ffn_parts.append((mine, swap_rep(mine)))
        low_parts.append((mine_low, swap_rep(mine_low)))
        hidden_parts.append(hidden_act)
        gate_parts.append(gate_grad)
        up_parts.append(up_grad)
    gate_grad = jnp.concatenate(gate_parts, axis=1)
    up_grad = jnp.concatenate(up_parts, axis=1)
    hidden_act = jnp.concatenate(hidden_parts, axis=1)
    normed_two_grad = sum_rows(
        low(
            contract(gate_grad, ffn_weight[:, 0, :], 1, 0)
            + contract(up_grad, ffn_weight[:, 1, :], 1, 0)
        ).reshape(micro, seq_len, model_dim)
    )
    normed_two_grad = normed_two_grad.reshape(count, model_dim).astype(jnp.float32)
    down_mine = sum_rows(
        jnp.concatenate(
            [
                low(contract(hidden_act, ffn_weight[:, 2, :], 1, 0)),
                low(contract(hidden_act, ffn_adapter, 1, 0)),
            ],
            axis=1,
        ).reshape(micro, seq_len, model_dim + RANK)
    ).reshape(count, model_dim + RANK)
    down_low = down_mine[:, model_dim:]
    result = (
        mixed_sum + down_mine[:, :model_dim].astype(jnp.float32) + contract(down_low, bd_t, 1, 1)
    )
    cot_full = cotangent.reshape(count, model_dim).astype(jnp.float32)
    mixed_part, gain_two_grad = norm_back_two(normed_two_grad)
    mixed_grad = cot_full + mixed_part
    out_grad_low = low(mixed_grad)
    out_cols = lax.all_to_all(
        out_grad_low.reshape(micro, local_len, model_dim), "fsdp", 2, 1, tiled=True
    ).reshape(every, attn_rows)
    wout_grad = contract(out_cols, kept_all[:, :q_width], 0, 0)
    context_grad = contract(out_grad_low, w_out, 1, 0)
    context_rows = low(context_grad).reshape(micro, local_len * HEADS, HD)
    prob_grad = batched(context_rows, values_all, 2, 2).reshape(micro, local_len, HEADS, seq_len)
    score_grad = weights * (prob_grad - jnp.sum(weights * prob_grad, axis=-1, keepdims=True))
    score_grad = low(score_grad).reshape(micro, local_len * HEADS, seq_len)
    query_grad = batched(score_grad, keys_all, 2, 1) * score_scale
    query_grad = query_grad.reshape(count, HEADS, HD)
    kv_grad = sum_rows(
        low(
            jnp.concatenate(
                [
                    batched(score_grad, queries, 1, 1) * score_scale,
                    batched(weights_low, context_rows, 1, 1),
                ],
                axis=2,
            )
        )
    ).reshape(count, 2 * HD)
    query_pre_grad = low(rotate(query_grad, -angles[:, None, :]).reshape(count, q_width))
    key_grad = low(rotate(kv_grad[:, :HD].astype(jnp.float32), -angles))
    value_grad = kv_grad[:, HD:]
    rank_grad = low(contract(query_pre_grad, bq_t, 1, 0))
    proj_grad = jnp.concatenate([query_pre_grad, key_grad, value_grad], axis=1)
    normed_grad = contract(proj_grad, w_proj, 1, 1) + contract(rank_grad, a_q, 1, 1)
    hidden_part, gain_one_grad = norm_back_one(normed_grad)
    input_grad = low(mixed_grad + hidden_part)
    back_all = gather_rows(
        jnp.concatenate([proj_grad, rank_grad, down_low], axis=1).reshape(
            micro, local_len, kv_end + 2 * RANK
        )
    ).reshape(every, kv_end + 2 * RANK)
    my_cols = me * attn_rows
    attn_in = contract(normed_cols, back_all[:, : kv_end + RANK], 0, 0)
    bq_grad = contract(
        lax.dynamic_slice_in_dim(back_all, my_cols, attn_rows, 1), kept_all[:, q_width:], 0, 0
    )
    bd_grad = contract(
        lax.dynamic_slice_in_dim(cot_all, my_cols, attn_rows, 1), back_all[:, kv_end + RANK :], 0, 0
    )
    gain_now = jnp.stack([gain_one_grad, gain_two_grad], axis=1).reshape(shards, attn_rows, 2)
    gain_now = lax.all_to_all(gain_now, "fsdp", 0, 0, tiled=True).sum(axis=0)
    tail = low(jnp.concatenate([attn_in, bq_grad, bd_grad], axis=1))
    tail_out = low(wout_grad)
    tail_gain = low(gain_now)

    def total(mine, other):
        return mine.astype(jnp.float32) + other.astype(jnp.float32)

    tail = total(tail, swap_rep(tail))
    tail_out = total(tail_out, swap_rep(tail_out))
    gains_grad = total(tail_gain, swap_rep(tail_gain))
    attn_grad = jnp.concatenate([tail[:, :kv_end], tail_out], axis=1)
    adapter_grad = tail[:, kv_end:]
    ffn_grad = jnp.concatenate([total(*pair) for pair in ffn_parts], axis=1).transpose(1, 0, 2)
    ffn_low_grad = jnp.concatenate([total(*pair) for pair in low_parts], axis=0)
    return (
        low(result).reshape(micro, local_len, model_dim),
        input_grad.reshape(micro, local_len, model_dim),
        gains_grad,
        attn_grad,
        adapter_grad,
        ffn_grad,
        ffn_low_grad,
    )


def solution(mesh):
    placed = (
        P("rep", "fsdp", None),
        P("rep", "fsdp"),
        P("fsdp", None),
        P("fsdp", None),
        P("fsdp", None),
        P("fsdp", None, None),
        P("fsdp", None),
        P("rep", "fsdp", None),
    )
    return jax.shard_map(
        local,
        mesh=mesh,
        in_specs=placed,
        out_specs=(
            P("rep", "fsdp", None),
            P("rep", "fsdp", None),
            P("fsdp", None),
            P("fsdp", None),
            P("fsdp", None),
            P("fsdp", None, None),
            P("fsdp", None),
        ),
        check_vma=False,
    )
```

profile of v0, /device:TPU:0, one launch (start us, length us, event | category | flops | bytes accessed | tf_op | source)
XLA Modules:
  0.0 1266.3 jit_solution(10089645762833557371)
XLA Ops:
  13.1 105.5 %all-gather.8.cloned.1.call-done = bf16[2048,3200]{1,0:T(8,128)(2,1)} async-done(((bf16[128,3200]{1,0:T(8,128)(2,1)}), bf16[2048,3200]{1,0:T(8,128)(2,1)}) %all-gather.8.cloned.1.call-update) | async-done | bytes 13107216 | tf_op jit(solution)/shard_map/all_gather | solution.py:66
  136.6 34.2 %all-gather.10.cloned.1.call-done = bf16[2,1024,512]{2,1,0:T(8,128)(2,1)} async-done(((bf16[2,64,512]{2,1,0:T(8,128)(2,1)}), bf16[2,1024,512]{2,1,0:T(8,128)(2,1)}) %all-gather.10.cloned.1.call-update) | async-done | bytes 2097168 | tf_op jit(solution)/shard_map/all_gather | solution.py:66
  178.1 75.3 %all-gather.12.cloned.1.call-done = bf16[2048,2304]{1,0:T(8,128)(2,1)} async-done(((bf16[128,2304]{1,0:T(8,128)(2,1)}), bf16[2048,2304]{1,0:T(8,128)(2,1)}) %all-gather.12.cloned.1.call-update) | async-done | bytes 9437200 | tf_op jit(solution)/shard_map/all_gather | solution.py:66
  253.4 6.4 multiply_reduce_fusion.1
  261.6 66.7 %all-gather.16.cloned.1.call-done = bf16[2,1024,2048]{2,1,0:T(8,128)(2,1)} async-done(((bf16[2,64,2048]{2,1,0:T(8,128)(2,1)}), bf16[2,1024,2048]{2,1,0:T(8,128)(2,1)}) %all-gather.16.cloned.1.call-update) | async-done | bytes 8388624 | tf_op jit(solution)/shard_map/all_gather | solution.py:66
  328.2 7.5 fusion.100
  354.1 49.7 %all-gather.14.cloned.1.call-done = bf16[2,1024,2048]{2,1,0:T(8,128)(2,1)} async-done(((bf16[2,64,2048]{2,1,0:T(8,128)(2,1)}), bf16[2,1024,2048]{2,1,0:T(8,128)(2,1)}) %all-gather.14.cloned.1.call-update) | async-done | bytes 8388624 | tf_op jit(solution)/shard_map/all_gather | solution.py:66
  403.8 7.6 fusion.110
  411.4 7.4 fusion.108
  450.8 14.4 %fusion.13 = f32[2048,2048]{1,0:T(8,128)} fusion(bf16[2048,256]{0,1:T(8,128)(2,1)} %get-tuple-element.27, bf16[2048,256]{0,1:T(8,128)(2,1)} %get-tuple-element.24, bf16[2048,256]{0,1:T(8,128)(2,1)} %get-tuple-element.21, bf16[2048,256]{0,1:T(8,128)(2,1)} %get-tuple-element.18, bf16[1024,3,2048]{2,0,1:T(8,128)(2,1)S(1)} %bitcast.272), kind=kOutput, calls=%fused_computation.22 | convolution fusion | flops 8606711808 | bytes 25165824 | tf_op jit(solution)/shard_map/dot_general | solution.py:44
  465.2 16.5 %add_convert_fusion = bf16[2048,2048]{1,0:T(8,128)(2,1)} fusion(f32[2048,2048]{1,0:T(8,128)} %fusion.13, bf16[2048,256]{0,1:T(8,128)(2,1)} %get-tuple-element.26, bf16[2048,256]{0,1:T(8,128)(2,1)} %get-tuple-element.23, bf16[2048,256]{0,1:T(8,128)(2,1)} %get-tuple-element.20, bf16[2048,256]{0,1:T(8,128)(2,1)S(1)} %copy-done.65, bf16[1024,3,2048]{2,0,1:T(8,128)(2,1)} %param.13), kind=kOutput, calls=%fused_computation.2 | convolution fusion | flops 8615100416 | bytes 33554432 | tf_op jit(solution)/shard_map/dot_general | solution.py:44
  481.7 13.9 %convolution_convert_fusion = bf16[2048,2048]{0,1:T(8,128)(2,1)} fusion(bf16[1024,3,2048]{2,0,1:T(8,128)(2,1)} %param.13, bf16[2048,256]{0,1:T(8,128)(2,1)S(1)} %get-tuple-element.28, bf16[2048,256]{0,1:T(8,128)(2,1)} %get-tuple-element.25, bf16[2048,256]{0,1:T(8,128)(2,1)} %get-tuple-element.22, bf16[2048,256]{0,1:T(8,128)(2,1)} %get-tuple-element.19), kind=kOutput, calls=%fused_computation.12 | convolution fusion | flops 8610906112 | bytes 16777216 | tf_op jit(solution)/shard_map/dot_general | solution.py:44
  495.6 88.2 %reduce-scatter.5.cloned.1.call-done = bf16[2,64,2048]{2,1,0:T(8,128)(2,1)} async-done(((bf16[2,1024,2048]{2,1,0:T(8,128)(2,1)}), bf16[2,64,2048]{2,1,0:T(8,128)(2,1)}) %reduce-scatter.5.cloned.1.call-update) | async-done | bytes 524304 | tf_op jit(solution)/shard_map/reduce_scatter | solution.py:70
  608.6 11.2 pad_maximum_fusion
  619.8 12.7 %copy.70 = bf16[2048,2304]{1,0:T(8,128)(2,1)} copy(bf16[2048,2304]{0,1:T(8,128)(2,1)} %pad_maximum_fusion) | data formatting | bytes 18874368 | tf_op jit(solution)/shard_map/reshape | solution.py:201
  638.4 64.7 %all-reduce.3.cloned.1.call-done = bf16[2,1024,512]{2,0,1:T(2,128)(2,1)} async-done(((bf16[2,1024,512]{2,0,1:T(2,128)(2,1)}), bf16[2,1024,512]{2,0,1:T(2,128)(2,1)}) %all-reduce.3.cloned.1.call-update) | async-done | bytes 2097168
  707.6 110.2 %reduce-scatter.3.cloned.1.call-done = bf16[2,64,2304]{2,1,0:T(8,128)(2,1)} async-done(((bf16[2,1024,2304]{2,1,0:T(8,128)(2,1)}), bf16[2,64,2304]{2,1,0:T(8,128)(2,1)}) %reduce-scatter.3.cloned.1.call-update) | async-done | bytes 589840 | tf_op jit(solution)/shard_map/reduce_scatter | solution.py:70
  826.5 21.9 %all-to-all-done.1 = bf16[16,2,8192]{2,1,0:T(2,128)(2,1)S(1)} async-done(((bf16[16,2,8192]{2,1,0:T(2,128)(2,1)}), bf16[16,2,8192]{2,1,0:T(2,128)(2,1)S(1)}, u32[]{:S(2)}, u32[]{:S(2)}) %all-to-all-start.1) | async-done | bytes 524320 | tf_op jit(solution)/shard_map/all_to_all | solution.py:118
  849.8 6.2 fusion.49
  856.0 5.9 fusion.48
  881.5 5.9 fusion.43
  893.3 6.1 fusion.41
  901.1 5.9 fusion.40
  907.0 6.1 fusion.39
  925.0 148.4 %collective-permute-done.10 = bf16[256,256]{1,0:T(8,128)(2,1)S(1)} collective-permute-done((bf16[256,256]{1,0:T(8,128)(2,1)S(1)}, bf16[256,256]{1,0:T(8,128)(2,1)S(1)}, u32[]{:S(2)}, u32[]{:S(2)}) %collective-permute-start.10) | collective-permute-done | bytes 131104 | tf_op jit(solution)/shard_map/ppermute | solution.py:74
  1074.8 67.5 %collective-permute-done.9 = bf16[256,256]{1,0:T(8,128)(2,1)S(1)} collective-permute-done((bf16[256,256]{1,0:T(8,128)(2,1)S(1)}, bf16[256,256]{1,0:T(8,128)(2,1)S(1)}, u32[]{:S(2)}, u32[]{:S(2)}) %collective-permute-start.9) | collective-permute-done | bytes 131104 | tf_op jit(solution)/shard_map/ppermute | solution.py:74
  1168.5 8.6 all-to-all-start.2
  1177.1 17.8 %maximum_bitcast_fusion = f32[1024,3,2048]{2,0,1:T(8,128)} fusion(f32[3,256,2048]{2,1,0:T(8,128)} %convert_add_fusion, f32[3,256,2048]{2,1,0:T(8,128)} %convert_add_fusion.1, f32[3,256,2048]{2,1,0:T(8,128)} %convert_add_fusion.2, f32[3,256,2048]{2,1,0:T(8,128)} %convert_add_fusion.3), kind=kLoop, calls=%fused_computation.1 | loop fusion | flops 18874368 | bytes 50331648 | tf_op jit(solution)/shard_map/transpose | solution.py:268
  1203.3 6.2 fusion.3
  1213.1 6.3 all-to-all-start
  1230.1 6.0 fusion.34
  1242.2 14.3 %collective-permute-done.1 = bf16[128,3328]{1,0:T(8,128)(2,1)S(1)} collective-permute-done((bf16[128,3328]{1,0:T(8,128)(2,1)S(1)}, bf16[128,3328]{1,0:T(8,128)(2,1)S(1)}, u32[]{:S(2)}, u32[]{:S(2)}) %collective-permute-start.1) | collective-permute-done | bytes 852000 | tf_op jit(solution)/shard_map/ppermute | solution.py:74
  (349 shorter events, 224.8 us)
Async XLA Ops:
  7.2 111.4 %all-gather.8.cloned.1.call-start = ((), (), s32[]{:S(2)}) async-start(), calls=%async_computation.5 | async-start | bytes 13926400 | tf_op jit(solution)/shard_map/all_gather | solution.py:66
  12.1 158.8 %all-gather.10.cloned.1.call-start = ((), (), s32[]{:S(2)}) async-start(), calls=%async_computation.6 | async-start | bytes 2228224 | tf_op jit(solution)/shard_map/all_gather | solution.py:66
  13.1 116.0 %copy-start.43 = (f32[128]{0:T(128)}, f32[128]{0:T(128)S(1)}, u32[]{:S(2)}) copy-start(f32[128]{0:T(128)S(1)} %multiply_power_fusion) | copy-start | bytes 1540
  120.6 465.1 %copy-start.33 = (f32[2048]{0:T(1024)}, f32[2048]{0:T(1024)S(1)}, u32[]{:S(2)}) copy-start(f32[2048]{0:T(1024)S(1)} %get-tuple-element.11) | copy-start | bytes 24580
  131.0 122.4 %all-gather.12.cloned.1.call-start = ((), (), s32[]{:S(2)}) async-start(), calls=%async_computation.7 | async-start | bytes 10027008 | tf_op jit(solution)/shard_map/all_gather | solution.py:66
  131.9 196.3 %all-gather.16.cloned.1.call-start = ((), (), s32[]{:S(2)}) async-start(), calls=%async_computation.10 | async-start | bytes 8912896 | tf_op jit(solution)/shard_map/all_gather | solution.py:66
  132.5 271.2 %all-gather.14.cloned.1.call-start = ((), (), s32[]{:S(2)}) async-start(), calls=%async_computation.8 | async-start | bytes 8912896 | tf_op jit(solution)/shard_map/all_gather | solution.py:66
  259.7 326.0 %copy-start = (f32[128,2048]{1,0:T(8,128)}, f32[128,2048]{1,0:T(8,128)S(1)}, u32[]{:S(2)}) copy-start(f32[128,2048]{1,0:T(8,128)S(1)} %get-tuple-element.48) | copy-start | bytes 3145732
  259.8 326.0 %copy-start.41 = (f32[128]{0:T(128)}, f32[128]{0:T(128)S(1)}, u32[]{:S(2)}) copy-start(f32[128]{0:T(128)S(1)} %fusion.176) | copy-start | bytes 1540
  261.0 322.8 %reduce-scatter.5.cloned.1.call-start = ((), (), s32[]{:S(2)}) async-start(), calls=%async_computation.11 | async-start | bytes 8912896 | tf_op jit(solution)/shard_map/reduce_scatter | solution.py:70
  440.6 164.6 %copy-start.18 = (bf16[2048,256]{0,1:T(8,128)(2,1)}, bf16[2048,256]{0,1:T(8,128)(2,1)S(1)}, u32[]{:S(2)}) copy-start(bf16[2048,256]{0,1:T(8,128)(2,1)S(1)} %get-tuple-element.28) | copy-start | bytes 3145732
  481.7 221.4 %all-reduce.3.cloned.1.call-start = ((), (), s32[]{:S(2)}) async-start(), calls=%async_computation.14 | async-start | bytes 4194304
  605.2 212.6 %reduce-scatter.3.cloned.1.call-start = ((), (), s32[]{:S(2)}) async-start(), calls=%async_computation.9 | async-start | bytes 10027008 | tf_op jit(solution)/shard_map/reduce_scatter | solution.py:70
  632.6 563.8 %all-gather.20.cloned.1.call-start = ((), (), s32[]{:S(2)}) async-start(), calls=%async_computation.13 | async-start | bytes 10027008 | tf_op jit(solution)/shard_map/all_gather | solution.py:66
  634.7 591.8 %all-gather.18.cloned.1.call-start = ((), (), s32[]{:S(2)}) async-start(), calls=%async_computation.12 | async-start | bytes 13369344 | tf_op jit(solution)/shard_map/all_gather | solution.py:66
  638.0 181.6 %copy-start.5 = (bf16[2,64,2048]{2,1,0:T(8,128)(2,1)S(1)}, bf16[2,64,2048]{2,1,0:T(8,128)(2,1)}, u32[]{:S(2)}) copy-start(bf16[2,64,2048]{2,1,0:T(8,128)(2,1)} %param.8) | copy-start | bytes 1572868
  638.0 181.6 %copy-start.36 = (f32[2048]{0:T(1024)S(1)}, f32[2048]{0:T(1024)}, u32[]{:S(2)}) copy-start(f32[2048]{0:T(1024)} %copy-done.35) | copy-start | bytes 24580
  638.0 181.6 %copy-start.52 = (f32[2,64]{1,0:T(2,128)S(1)}, f32[2,64]{1,0:T(2,128)}, u32[]{:S(2)}) copy-start(f32[2,64]{1,0:T(2,128)} %get-tuple-element.37) | copy-start | bytes 1540
  822.1 26.2 %all-to-all-start.1 = ((bf16[16,2,8192]{2,1,0:T(2,128)(2,1)}), bf16[16,2,8192]{2,1,0:T(2,128)(2,1)S(1)}, u32[]{:S(2)}, u32[]{:S(2)}) async-start(bf16[16,2,8192]{2,1,0:T(2,128)(2,1)} %reshape.417), calls=%async_computation.3 | async-start | bytes 1048576 | tf_op jit(solution)/shard_map/all_to_all | solution.py:118
  864.7 288.7 %collective-permute-start.6 = (bf16[3,256,2048]{2,1,0:T(8,128)(2,1)S(1)}, bf16[3,256,2048]{2,1,0:T(8,128)(2,1)S(1)}, u32[]{:S(2)}, u32[]{:S(2)}) collective-permute-start(bf16[3,256,2048]{2,1,0:T(8,128)(2,1)S(1)} %pad_maximum_fusion.5), channel_id=1, source_target_pairs={{0,16},{16,0},{1,17},{17,1},{2,18},{18,2},{3,19},{19,3},{4,20},{20... | collective-permute-start | bytes 9437192 | tf_op jit(solution)/shard_map/ppermute | solution.py:74
  880.6 276.0 %collective-permute-start.5 = (bf16[3,256,2048]{2,1,0:T(8,128)(2,1)S(1)}, bf16[3,256,2048]{2,1,0:T(8,128)(2,1)S(1)}, u32[]{:S(2)}, u32[]{:S(2)}) collective-permute-start(bf16[3,256,2048]{2,1,0:T(8,128)(2,1)S(1)} %pad_maximum_fusion.4), channel_id=1, source_target_pairs={{0,16},{16,0},{1,17},{17,1},{2,18},{18,2},{3,19},{19,3},{4,20},{20... | collective-permute-start | bytes 9437192 | tf_op jit(solution)/shard_map/ppermute | solution.py:74
  899.7 260.1 %collective-permute-start.4 = (bf16[3,256,2048]{2,1,0:T(8,128)(2,1)S(1)}, bf16[3,256,2048]{2,1,0:T(8,128)(2,1)S(1)}, u32[]{:S(2)}, u32[]{:S(2)}) collective-permute-start(bf16[3,256,2048]{2,1,0:T(8,128)(2,1)S(1)} %pad_maximum_fusion.3), channel_id=1, source_target_pairs={{0,16},{16,0},{1,17},{17,1},{2,18},{18,2},{3,19},{19,3},{4,20},{20... | collective-permute-start | bytes 9437192 | tf_op jit(solution)/shard_map/ppermute | solution.py:74
  920.6 152.8 %collective-permute-start.10 = (bf16[256,256]{1,0:T(8,128)(2,1)S(1)}, bf16[256,256]{1,0:T(8,128)(2,1)S(1)}, u32[]{:S(2)}, u32[]{:S(2)}) collective-permute-start(bf16[256,256]{1,0:T(8,128)(2,1)S(1)} %convolution_convert_fusion.17), channel_id=1, source_target_pairs={{0,16},{16,0},{1,17},{17,1},{2,18},{18,2},{3,19},{19,3},{4,20},{20... | collective-permute-start | bytes 393224 | tf_op jit(solution)/shard_map/ppermute | solution.py:74
  923.5 239.5 %collective-permute-start.3 = (bf16[3,256,2048]{2,1,0:T(8,128)(2,1)S(1)}, bf16[3,256,2048]{2,1,0:T(8,128)(2,1)S(1)}, u32[]{:S(2)}, u32[]{:S(2)}) collective-permute-start(bf16[3,256,2048]{2,1,0:T(8,128)(2,1)S(1)} %pad_maximum_fusion.2), channel_id=1, source_target_pairs={{0,16},{16,0},{1,17},{17,1},{2,18},{18,2},{3,19},{19,3},{4,20},{20... | collective-permute-start | bytes 9437192 | tf_op jit(solution)/shard_map/ppermute | solution.py:74
  1073.3 69.0 %collective-permute-start.9 = (bf16[256,256]{1,0:T(8,128)(2,1)S(1)}, bf16[256,256]{1,0:T(8,128)(2,1)S(1)}, u32[]{:S(2)}, u32[]{:S(2)}) collective-permute-start(bf16[256,256]{1,0:T(8,128)(2,1)S(1)} %convolution_convert_fusion.18), channel_id=1, source_target_pairs={{0,16},{16,0},{1,17},{17,1},{2,18},{18,2},{3,19},{19,3},{4,20},{20... | collective-permute-start | bytes 393224 | tf_op jit(solution)/shard_map/ppermute | solution.py:74
  1142.4 5.0 collective-permute-start.8
  1147.3 5.0 collective-permute-start.7
  1168.5 26.4 %all-to-all-start.2 = ((bf16[16,2,8192]{2,1,0:T(2,128)(2,1)}), bf16[16,2,8192]{2,1,0:T(2,128)(2,1)S(1)}, u32[]{:S(2)}, u32[]{:S(2)}) async-start(bf16[16,2,8192]{2,1,0:T(2,128)(2,1)} %reshape.415), calls=%async_computation.4 | async-start | bytes 1048576 | tf_op jit(solution)/shard_map/all_to_all | solution.py:211
  1201.8 36.4 %collective-permute-start.2 = (bf16[128,2048]{1,0:T(8,128)(2,1)}, bf16[128,2048]{1,0:T(8,128)(2,1)}, u32[]{:S(2)}, u32[]{:S(2)}) collective-permute-start(bf16[128,2048]{1,0:T(8,128)(2,1)} %fusion.56), channel_id=1, source_target_pairs={{0,16},{16,0},{1,17},{17,1},{2,18},{18,2},{3,19},{19,3},{4,20},{20... | collective-permute-start | bytes 1572872 | tf_op jit(solution)/shard_map/ppermute | solution.py:74
  1213.1 12.8 %all-to-all-start = ((f32[16,128,2]{1,2,0:T(2,128)}), f32[16,128,2]{1,2,0:T(2,128)S(1)}, u32[]{:S(2)}, u32[]{:S(2)}) async-start(f32[16,128,2]{1,2,0:T(2,128)} %copy.61), calls=%async_computation.2 | async-start | bytes 32768 | tf_op jit(solution)/shard_map/all_to_all | solution.py:255
  1225.9 11.8 collective-permute-start
  1236.1 20.4 %collective-permute-start.1 = (bf16[128,3328]{1,0:T(8,128)(2,1)S(1)}, bf16[128,3328]{1,0:T(8,128)(2,1)S(1)}, u32[]{:S(2)}, u32[]{:S(2)}) collective-permute-start(bf16[128,3328]{1,0:T(8,128)(2,1)S(1)} %pad_maximum_fusion.9), channel_id=1, source_target_pairs={{0,16},{16,0},{1,17},{17,1},{2,18},{18,2},{3,19},{19,3},{4,20},{20... | collective-permute-start | bytes 2555912 | tf_op jit(solution)/shard_map/ppermute | solution.py:74
  (76 other events, 1120.7 us)
Sparse Core Ops, SparseCore 0:
  12.2 106.3 all-gather.7
  131.1 39.7 all-gather.9
  173.7 79.6 all-gather.11
  255.4 72.7 all-gather.15
  330.8 72.8 all-gather.13
  481.8 101.9 reduce-scatter.4
  605.4 97.6 all-reduce.2
  707.2 110.6 reduce-scatter.2
  820.1 90.3 all-gather.19
  912.7 98.8 all-gather.17
where the time goes:
time: 1280 us; the launch traced here: 1270 us
  waiting for transfers between devices  858 us (67%)
  matrix products  246 us (19%)
  other arithmetic  69.1 us (5%)
  local copies, waits for them, and re-layouts  42.9 us (3%)
  starting transfers between devices  34.2 us (3%)
  between operations  16.7 us (1%)
    all_gather x7, waiting for transfers between devices, gather_rows(): return lax.all_gather(values, 'fsdp', axis=values.ndim - 2, tiled=True)  331 us
    ppermute x11, waiting for transfers between devices, swap_rep(): return lax.ppermute(values, 'rep', [(0, 1), (1, 0)])  237 us
    dot_general x50, matrix products, contract(): lax.dot_general(left_op, right_op, (((left_dim,), (right_dim,)), ((), ())...  236 us
    reduce_scatter x2, waiting for transfers between devices, sum_rows(): return lax.psum_scatter(values, 'fsdp', scatter_dimension=1, tiled=True)  198 us
    unnamed x11, waiting for transfers between devices  65.3 us
  transfers between devices with their start and end apart: 24, of which 15 were waited for; matrix products, arithmetic and copies ran while one was open for 19% of the time, Pallas kernels for 0%

commit v1 on v0

--- a/solution.py
+++ b/solution.py
@@ -1,3 +1,4 @@
+import functools
 import jax
 import jax.numpy as jnp
 from jax import lax
@@ -8,6 +9,30 @@
 RANK = 256
 CHUNKS = 4
 epsilon = 1e-06
+
+
+def check_terms(piece_in, at_axis, axis_no):
+    current_arr = jax.lax.axis_size("fsdp")
+    u_next, big = (current_arr, jax.lax.axis_index("fsdp"))
+    latest = list(piece_in.shape)
+    raw_out = piece_in.shape[at_axis] // u_next
+    latest[at_axis] = raw_out
+    val2 = latest[axis_no]
+    latest[axis_no] = val2 * u_next
+    side_arr = jnp.zeros(latest, piece_in.dtype)
+    for jj in range(u_next):
+        answer = lax.dynamic_slice_in_dim(piece_in, (big ^ jj) * raw_out, raw_out, axis=at_axis)
+        if jj:
+            answer = jax.lax.ppermute(
+                answer, axis_name="fsdp", perm=[(src_i, src_i ^ jj) for src_i in range(u_next)]
+            )
+        side_arr = lax.dynamic_update_slice_in_dim(
+            side_arr, answer, (big ^ jj) * val2, axis=axis_no
+        )
+    return side_arr
+
+
+meet_blocks = functools.partial(check_terms, at_axis=2, axis_no=1)
 
 
 def rms_scale(values, gain_col):
@@ -115,9 +140,9 @@
     angles = angles_of(query_index[None, :] - before).reshape(count, HD // 2)
     normed, norm_back_one = jax.vjp(rms_scale, hidden_in, gain_two[:, 0])
     normed_low = low(normed)
-    normed_cols = lax.all_to_all(
-        normed_low.reshape(micro, local_len, model_dim), "fsdp", 2, 1, tiled=True
-    ).reshape(every, attn_rows)
+    normed_cols = meet_blocks(normed_low.reshape(micro, local_len, model_dim)).reshape(
+        every, attn_rows
+    )
     projected = contract(normed_low, w_proj, 1, 0)
     query_low = low(contract(normed_low, a_q, 1, 0))
     query_pre = projected[:, :q_width] + contract(query_low, bq_t, 1, 1)

time: 1280 us -> 1280 us (level)
  starting transfers between devices: 34.2 us -> 55.9 us
  waiting for transfers between devices: 858 us -> 839 us
    ppermute x0 -> x15, starting transfers between devices: none -> 24.7 us  [check_terms(): jax.lax.ppermute(answer, axis_name='fsdp', perm=[(src_i, src_i ^ jj) for...]
    all_to_all x1 -> x0, waiting for transfers between devices: 21.9 us -> none  [local(): lax.all_to_all(normed_low.reshape(micro, local_len, model_dim), 'fsdp', 2...]
  transfers between devices with their start and end apart: 24 -> 38, of which waited for: 15 -> 17; matrix products, arithmetic and copies ran while one was open for 19% -> 18% of each run, Pallas kernels for 0% -> 0%
where the time goes in v1:
time: 1280 us; the launch traced here: 1270 us
  waiting for transfers between devices  839 us (66%)
  matrix products  246 us (19%)
  other arithmetic  68.7 us (5%)
  starting transfers between devices  55.9 us (4%)
  local copies, waits for them, and re-layouts  39.6 us (3%)
  between operations  17.1 us (1%)
    all_gather x7, waiting for transfers between devices, gather_rows(): return lax.all_gather(values, 'fsdp', axis=values.ndim - 2, tiled=True)  331 us
    ppermute x11, waiting for transfers between devices, swap_rep(): return lax.ppermute(values, 'rep', [(0, 1), (1, 0)])  236 us
    dot_general x50, matrix products, contract(): lax.dot_general(left_op, right_op, (((left_dim,), (right_dim,)), ((), ())...  236 us
    reduce_scatter x2, waiting for transfers between devices, sum_rows(): return lax.psum_scatter(values, 'fsdp', scatter_dimension=1, tiled=True)  198 us
    unnamed x11, waiting for transfers between devices  64.5 us
  transfers between devices with their start and end apart: 38, of which 17 were waited for; matrix products, arithmetic and copies ran while one was open for 18% of the time, Pallas kernels for 0%

profile of v1, /device:TPU:0, one launch (start us, length us, event | category | flops | bytes accessed | tf_op | source)
XLA Modules:
  0.0 1266.5 jit_solution(8313815986486152845)
XLA Ops:
  13.1 105.5 %all-gather.8.cloned.1.call-done = bf16[2048,3200]{1,0:T(8,128)(2,1)} async-done(((bf16[128,3200]{1,0:T(8,128)(2,1)}), bf16[2048,3200]{1,0:T(8,128)(2,1)}) %all-gather.8.cloned.1.call-update) | async-done | bytes 13107216 | tf_op jit(solution)/shard_map/all_gather | solution.py:91
  136.6 34.2 %all-gather.10.cloned.1.call-done = bf16[2,1024,512]{2,1,0:T(8,128)(2,1)} async-done(((bf16[2,64,512]{2,1,0:T(8,128)(2,1)}), bf16[2,1024,512]{2,1,0:T(8,128)(2,1)}) %all-gather.10.cloned.1.call-update) | async-done | bytes 2097168 | tf_op jit(solution)/shard_map/all_gather | solution.py:91
  178.1 75.3 %all-gather.12.cloned.1.call-done = bf16[2048,2304]{1,0:T(8,128)(2,1)} async-done(((bf16[128,2304]{1,0:T(8,128)(2,1)}), bf16[2048,2304]{1,0:T(8,128)(2,1)}) %all-gather.12.cloned.1.call-update) | async-done | bytes 9437200 | tf_op jit(solution)/shard_map/all_gather | solution.py:91
  253.4 6.4 multiply_reduce_fusion.1
  261.5 66.7 %all-gather.16.cloned.1.call-done = bf16[2,1024,2048]{2,1,0:T(8,128)(2,1)} async-done(((bf16[2,64,2048]{2,1,0:T(8,128)(2,1)}), bf16[2,1024,2048]{2,1,0:T(8,128)(2,1)}) %all-gather.16.cloned.1.call-update) | async-done | bytes 8388624 | tf_op jit(solution)/shard_map/all_gather | solution.py:91
  328.2 7.5 fusion.100
  354.1 49.6 %all-gather.14.cloned.1.call-done = bf16[2,1024,2048]{2,1,0:T(8,128)(2,1)} async-done(((bf16[2,64,2048]{2,1,0:T(8,128)(2,1)}), bf16[2,1024,2048]{2,1,0:T(8,128)(2,1)}) %all-gather.14.cloned.1.call-update) | async-done | bytes 8388624 | tf_op jit(solution)/shard_map/all_gather | solution.py:91
  403.7 7.6 fusion.110
  411.4 7.4 fusion.108
  450.8 14.4 %fusion.13 = f32[2048,2048]{1,0:T(8,128)} fusion(bf16[2048,256]{0,1:T(8,128)(2,1)} %get-tuple-element.27, bf16[2048,256]{0,1:T(8,128)(2,1)} %get-tuple-element.24, bf16[2048,256]{0,1:T(8,128)(2,1)} %get-tuple-element.21, bf16[2048,256]{0,1:T(8,128)(2,1)} %get-tuple-element.18, bf16[1024,3,2048]{2,0,1:T(8,128)(2,1)S(1)} %bitcast.264), kind=kOutput, calls=%fused_computation.22 | convolution fusion | flops 8606711808 | bytes 25165824 | tf_op jit(solution)/shard_map/dot_general | solution.py:69
  465.1 16.3 %add_convert_fusion = bf16[2048,2048]{1,0:T(8,128)(2,1)} fusion(f32[2048,2048]{1,0:T(8,128)} %fusion.13, bf16[2048,256]{0,1:T(8,128)(2,1)} %get-tuple-element.26, bf16[2048,256]{0,1:T(8,128)(2,1)} %get-tuple-element.23, bf16[2048,256]{0,1:T(8,128)(2,1)} %get-tuple-element.20, bf16[2048,256]{0,1:T(8,128)(2,1)S(1)} %copy-done.66, bf16[1024,3,2048]{2,0,1:T(8,128)(2,1)} %param.13), kind=kOutput, calls=%fused_computation.2 | convolution fusion | flops 8615100416 | bytes 33554432 | tf_op jit(solution)/shard_map/dot_general | solution.py:69
  481.5 14.0 %convolution_convert_fusion = bf16[2048,2048]{0,1:T(8,128)(2,1)} fusion(bf16[1024,3,2048]{2,0,1:T(8,128)(2,1)} %param.13, bf16[2048,256]{0,1:T(8,128)(2,1)S(1)} %get-tuple-element.28, bf16[2048,256]{0,1:T(8,128)(2,1)} %get-tuple-element.25, bf16[2048,256]{0,1:T(8,128)(2,1)} %get-tuple-element.22, bf16[2048,256]{0,1:T(8,128)(2,1)} %get-tuple-element.19), kind=kOutput, calls=%fused_computation.12 | convolution fusion | flops 8610906112 | bytes 16777216 | tf_op jit(solution)/shard_map/dot_general | solution.py:69
  495.5 88.1 %reduce-scatter.5.cloned.1.call-done = bf16[2,64,2048]{2,1,0:T(8,128)(2,1)} async-done(((bf16[2,1024,2048]{2,1,0:T(8,128)(2,1)}), bf16[2,64,2048]{2,1,0:T(8,128)(2,1)}) %reduce-scatter.5.cloned.1.call-update) | async-done | bytes 524304 | tf_op jit(solution)/shard_map/reduce_scatter | solution.py:95
  607.8 10.8 pad_maximum_fusion
  618.5 12.8 %copy.50 = bf16[2048,2304]{1,0:T(8,128)(2,1)} copy(bf16[2048,2304]{0,1:T(8,128)(2,1)} %pad_maximum_fusion) | data formatting | bytes 18874368 | tf_op jit(solution)/shard_map/reshape | solution.py:226
  638.3 63.9 %all-reduce.3.cloned.1.call-done = bf16[2,1024,512]{2,0,1:T(2,128)(2,1)} async-done(((bf16[2,1024,512]{2,0,1:T(2,128)(2,1)}), bf16[2,1024,512]{2,0,1:T(2,128)(2,1)}) %all-reduce.3.cloned.1.call-update) | async-done | bytes 2097168
  706.7 110.2 %reduce-scatter.3.cloned.1.call-done = bf16[2,64,2304]{2,1,0:T(8,128)(2,1)} async-done(((bf16[2,1024,2304]{2,1,0:T(8,128)(2,1)}), bf16[2,64,2304]{2,1,0:T(8,128)(2,1)}) %reduce-scatter.3.cloned.1.call-update) | async-done | bytes 589840 | tf_op jit(solution)/shard_map/reduce_scatter | solution.py:95
  836.7 6.0 collective-permute-start.14
  849.6 5.9 fusion.49
  855.6 5.9 fusion.48
  868.5 6.0 fusion.45
  887.3 5.9 fusion.42
  893.2 6.1 fusion.41
  906.9 6.3 fusion.39
  924.9 148.0 %collective-permute-done.25 = bf16[256,256]{1,0:T(8,128)(2,1)S(1)} collective-permute-done((bf16[256,256]{1,0:T(8,128)(2,1)S(1)}, bf16[256,256]{1,0:T(8,128)(2,1)S(1)}, u32[]{:S(2)}, u32[]{:S(2)}) %collective-permute-start.25) | collective-permute-done | bytes 131104 | tf_op jit(solution)/shard_map/ppermute | solution.py:99
  1074.7 67.5 %collective-permute-done.24 = bf16[256,256]{1,0:T(8,128)(2,1)S(1)} collective-permute-done((bf16[256,256]{1,0:T(8,128)(2,1)S(1)}, bf16[256,256]{1,0:T(8,128)(2,1)S(1)}, u32[]{:S(2)}, u32[]{:S(2)}) %collective-permute-start.24) | collective-permute-done | bytes 131104 | tf_op jit(solution)/shard_map/ppermute | solution.py:99
  1168.5 8.8 all-to-all-start.1
  1177.3 17.8 %maximum_bitcast_fusion = f32[1024,3,2048]{2,0,1:T(8,128)} fusion(f32[3,256,2048]{2,1,0:T(8,128)} %convert_add_fusion, f32[3,256,2048]{2,1,0:T(8,128)} %convert_add_fusion.1, f32[3,256,2048]{2,1,0:T(8,128)} %convert_add_fusion.2, f32[3,256,2048]{2,1,0:T(8,128)} %convert_add_fusion.3), kind=kLoop, calls=%fused_computation.1 | loop fusion | flops 18874368 | bytes 50331648 | tf_op jit(solution)/shard_map/transpose | solution.py:293
  1203.6 6.2 fusion.3
  1213.3 6.1 all-to-all-start
  1230.1 6.0 fusion.34
  1242.3 14.3 %collective-permute-done.16 = bf16[128,3328]{1,0:T(8,128)(2,1)S(1)} collective-permute-done((bf16[128,3328]{1,0:T(8,128)(2,1)S(1)}, bf16[128,3328]{1,0:T(8,128)(2,1)S(1)}, u32[]{:S(2)}, u32[]{:S(2)}) %collective-permute-start.16) | collective-permute-done | bytes 852000 | tf_op jit(solution)/shard_map/ppermute | solution.py:99
  (392 shorter events, 242.0 us)
Async XLA Ops:
  7.2 111.4 %all-gather.8.cloned.1.call-start = ((), (), s32[]{:S(2)}) async-start(), calls=%async_computation.4 | async-start | bytes 13926400 | tf_op jit(solution)/shard_map/all_gather | solution.py:91
  12.1 158.8 %all-gather.10.cloned.1.call-start = ((), (), s32[]{:S(2)}) async-start(), calls=%async_computation.5 | async-start | bytes 2228224 | tf_op jit(solution)/shard_map/all_gather | solution.py:91
  131.0 122.4 %all-gather.12.cloned.1.call-start = ((), (), s32[]{:S(2)}) async-start(), calls=%async_computation.6 | async-start | bytes 10027008 | tf_op jit(solution)/shard_map/all_gather | solution.py:91
  131.9 196.3 %all-gather.16.cloned.1.call-start = ((), (), s32[]{:S(2)}) async-start(), calls=%async_computation.9 | async-start | bytes 8912896 | tf_op jit(solution)/shard_map/all_gather | solution.py:91
  132.5 271.2 %all-gather.14.cloned.1.call-start = ((), (), s32[]{:S(2)}) async-start(), calls=%async_computation.7 | async-start | bytes 8912896 | tf_op jit(solution)/shard_map/all_gather | solution.py:91
  261.0 322.6 %reduce-scatter.5.cloned.1.call-start = ((), (), s32[]{:S(2)}) async-start(), calls=%async_computation.10 | async-start | bytes 8912896 | tf_op jit(solution)/shard_map/reduce_scatter | solution.py:95
  481.4 220.7 %all-reduce.3.cloned.1.call-start = ((), (), s32[]{:S(2)}) async-start(), calls=%async_computation.13 | async-start | bytes 4194304
  604.3 212.7 %reduce-scatter.3.cloned.1.call-start = ((), (), s32[]{:S(2)}) async-start(), calls=%async_computation.8 | async-start | bytes 10027008 | tf_op jit(solution)/shard_map/reduce_scatter | solution.py:95
  631.4 565.1 %all-gather.20.cloned.1.call-start = ((), (), s32[]{:S(2)}) async-start(), calls=%async_computation.12 | async-start | bytes 10027008 | tf_op jit(solution)/shard_map/all_gather | solution.py:91
  633.6 593.0 %all-gather.18.cloned.1.call-start = ((), (), s32[]{:S(2)}) async-start(), calls=%async_computation.11 | async-start | bytes 13369344 | tf_op jit(solution)/shard_map/all_gather | solution.py:91
  821.8 6.6 collective-permute-start.4
  823.6 8.6 collective-permute-start.6
  826.2 6.7 collective-permute-start.7
  826.3 8.6 collective-permute-start.8
  828.5 8.2 collective-permute-start.9
  829.3 13.9 %collective-permute-start.10 = (bf16[2,64,128]{2,1,0:T(8,128)(2,1)}, bf16[2,64,128]{2,1,0:T(8,128)(2,1)S(1)}, u32[]{:S(2)}, u32[]{:S(2)}) collective-permute-start(bf16[2,64,128]{2,1,0:T(8,128)(2,1)} %get-tuple-element.40), channel_id=1, source_target_pairs={{0,10},{1,11},{2,8},{3,9},{4,14},{5,15},{6,12},{7,13},{8,2},{9,3},... | collective-permute-start | bytes 98312 | tf_op jit(solution)/shard_map/ppermute | solution.py:26
  832.2 14.2 %collective-permute-start.11 = (bf16[2,64,128]{2,1,0:T(8,128)(2,1)}, bf16[2,64,128]{2,1,0:T(8,128)(2,1)S(1)}, u32[]{:S(2)}, u32[]{:S(2)}) collective-permute-start(bf16[2,64,128]{2,1,0:T(8,128)(2,1)} %get-tuple-element.39), channel_id=1, source_target_pairs={{0,11},{1,10},{2,9},{3,8},{4,15},{5,14},{6,13},{7,12},{8,3},{9,2},... | collective-permute-start | bytes 98312 | tf_op jit(solution)/shard_map/ppermute | solution.py:26
  832.8 13.6 %collective-permute-start.12 = (bf16[2,64,128]{2,1,0:T(8,128)(2,1)}, bf16[2,64,128]{2,1,0:T(8,128)(2,1)S(1)}, u32[]{:S(2)}, u32[]{:S(2)}) collective-permute-start(bf16[2,64,128]{2,1,0:T(8,128)(2,1)} %get-tuple-element.38), channel_id=1, source_target_pairs={{0,12},{1,13},{2,14},{3,15},{4,8},{5,9},{6,10},{7,11},{8,4},{9,5},... | collective-permute-start | bytes 98312 | tf_op jit(solution)/shard_map/ppermute | solution.py:26
  835.0 11.5 collective-permute-start.13
  836.7 9.8 collective-permute-start.14
  843.2 6.4 collective-permute-start.15
  864.2 289.1 %collective-permute-start.21 = (bf16[3,256,2048]{2,1,0:T(8,128)(2,1)S(1)}, bf16[3,256,2048]{2,1,0:T(8,128)(2,1)S(1)}, u32[]{:S(2)}, u32[]{:S(2)}) collective-permute-start(bf16[3,256,2048]{2,1,0:T(8,128)(2,1)S(1)} %pad_maximum_fusion.5), channel_id=1, source_target_pairs={{0,16},{16,0},{1,17},{17,1},{2,18},{18,2},{3,19},{19,3},{4,20},{20... | collective-permute-start | bytes 9437192 | tf_op jit(solution)/shard_map/ppermute | solution.py:99
  880.7 275.9 %collective-permute-start.20 = (bf16[3,256,2048]{2,1,0:T(8,128)(2,1)S(1)}, bf16[3,256,2048]{2,1,0:T(8,128)(2,1)S(1)}, u32[]{:S(2)}, u32[]{:S(2)}) collective-permute-start(bf16[3,256,2048]{2,1,0:T(8,128)(2,1)S(1)} %pad_maximum_fusion.4), channel_id=1, source_target_pairs={{0,16},{16,0},{1,17},{17,1},{2,18},{18,2},{3,19},{19,3},{4,20},{20... | collective-permute-start | bytes 9437192 | tf_op jit(solution)/shard_map/ppermute | solution.py:99
  899.7 260.1 %collective-permute-start.19 = (bf16[3,256,2048]{2,1,0:T(8,128)(2,1)S(1)}, bf16[3,256,2048]{2,1,0:T(8,128)(2,1)S(1)}, u32[]{:S(2)}, u32[]{:S(2)}) collective-permute-start(bf16[3,256,2048]{2,1,0:T(8,128)(2,1)S(1)} %pad_maximum_fusion.3), channel_id=1, source_target_pairs={{0,16},{16,0},{1,17},{17,1},{2,18},{18,2},{3,19},{19,3},{4,20},{20... | collective-permute-start | bytes 9437192 | tf_op jit(solution)/shard_map/ppermute | solution.py:99
  920.7 152.2 %collective-permute-start.25 = (bf16[256,256]{1,0:T(8,128)(2,1)S(1)}, bf16[256,256]{1,0:T(8,128)(2,1)S(1)}, u32[]{:S(2)}, u32[]{:S(2)}) collective-permute-start(bf16[256,256]{1,0:T(8,128)(2,1)S(1)} %convolution_convert_fusion.17), channel_id=1, source_target_pairs={{0,16},{16,0},{1,17},{17,1},{2,18},{18,2},{3,19},{19,3},{4,20},{20... | collective-permute-start | bytes 393224 | tf_op jit(solution)/shard_map/ppermute | solution.py:99
  923.4 239.6 %collective-permute-start.18 = (bf16[3,256,2048]{2,1,0:T(8,128)(2,1)S(1)}, bf16[3,256,2048]{2,1,0:T(8,128)(2,1)S(1)}, u32[]{:S(2)}, u32[]{:S(2)}) collective-permute-start(bf16[3,256,2048]{2,1,0:T(8,128)(2,1)S(1)} %pad_maximum_fusion.2), channel_id=1, source_target_pairs={{0,16},{16,0},{1,17},{17,1},{2,18},{18,2},{3,19},{19,3},{4,20},{20... | collective-permute-start | bytes 9437192 | tf_op jit(solution)/shard_map/ppermute | solution.py:99
  1072.9 69.4 %collective-permute-start.24 = (bf16[256,256]{1,0:T(8,128)(2,1)S(1)}, bf16[256,256]{1,0:T(8,128)(2,1)S(1)}, u32[]{:S(2)}, u32[]{:S(2)}) collective-permute-start(bf16[256,256]{1,0:T(8,128)(2,1)S(1)} %convolution_convert_fusion.18), channel_id=1, source_target_pairs={{0,16},{16,0},{1,17},{17,1},{2,18},{18,2},{3,19},{19,3},{4,20},{20... | collective-permute-start | bytes 393224 | tf_op jit(solution)/shard_map/ppermute | solution.py:99
  1168.5 26.6 %all-to-all-start.1 = ((bf16[16,2,8192]{2,1,0:T(2,128)(2,1)}), bf16[16,2,8192]{2,1,0:T(2,128)(2,1)S(1)}, u32[]{:S(2)}, u32[]{:S(2)}) async-start(bf16[16,2,8192]{2,1,0:T(2,128)(2,1)} %reshape.414), calls=%async_computation.3 | async-start | bytes 1048576 | tf_op jit(solution)/shard_map/all_to_all | solution.py:236
  1202.1 36.2 %collective-permute-start.17 = (bf16[128,2048]{1,0:T(8,128)(2,1)}, bf16[128,2048]{1,0:T(8,128)(2,1)}, u32[]{:S(2)}, u32[]{:S(2)}) collective-permute-start(bf16[128,2048]{1,0:T(8,128)(2,1)} %fusion.56), channel_id=1, source_target_pairs={{0,16},{16,0},{1,17},{17,1},{2,18},{18,2},{3,19},{19,3},{4,20},{20... | collective-permute-start | bytes 1572872 | tf_op jit(solution)/shard_map/ppermute | solution.py:99
  1213.3 12.6 all-to-all-start
  1226.0 11.8 collective-permute-start
  1236.2 20.4 %collective-permute-start.16 = (bf16[128,3328]{1,0:T(8,128)(2,1)S(1)}, bf16[128,3328]{1,0:T(8,128)(2,1)S(1)}, u32[]{:S(2)}, u32[]{:S(2)}) collective-permute-start(bf16[128,3328]{1,0:T(8,128)(2,1)S(1)} %pad_maximum_fusion.9), channel_id=1, source_target_pairs={{0,16},{16,0},{1,17},{17,1},{2,18},{18,2},{3,19},{19,3},{4,20},{20... | collective-permute-start | bytes 2555912 | tf_op jit(solution)/shard_map/ppermute | solution.py:99
  (91 other events, 3374.6 us)
Sparse Core Ops, SparseCore 0:
  12.2 106.3 all-gather.7
  131.1 39.7 all-gather.9
  173.7 79.6 all-gather.11
  255.4 72.7 all-gather.15
  330.8 72.8 all-gather.13
  481.6 101.9 reduce-scatter.4
  604.4 97.7 all-reduce.2
  706.3 110.6 reduce-scatter.2
  819.2 91.7 all-gather.19
  913.2 98.6 all-gather.17
